TPU v7x, 32 devices: a whole 2x2x4 slice. The times are simulated.
32 devices in a mesh: dp: 8 (over y, x, core), ctx: 4 (over z).
Axes of the slice: x: 2, y: 2, z: 4, core: 2. Of those that a mesh axis runs over, the one named last changes fastest.
Arguments:
- inputs: bfloat16 [8, 1024, 2048], P('dp', 'ctx'), may hold values from -6 to 6
- lengths: int32 [8], P('dp'), may hold values from 512 to 1024, as said below
- norm_gain: bfloat16 [2048], replicated, may hold values from 0.5 to 1.5
- up_weight: bfloat16 [2048, 8192], P('dp'), may hold values from -0.125 to 0.125
- conv_weight: bfloat16 [4, 4096], replicated, may hold values from -3 to 3
- conv_bias: bfloat16 [4096], replicated, may hold values from -3 to 3
- qkv_weight: bfloat16 [3, 4, 4, 4, 256], replicated, may hold values from -3 to 3
- gate_weight: bfloat16 [8, 12288], replicated, may hold values from -0.109375 to 0.109375
- gate_bias: bfloat16 [8], replicated, may hold values from -1 to 8.5
- skip_weight: bfloat16 [4096], replicated, may hold values from 0.5 to 1.5
- outnorm_weight: bfloat16 [4096], replicated, may hold values from 0.5 to 1.5
- down_weight: bfloat16 [4096, 2048], P('dp'), may hold values from -0.09375 to 0.09375
- grad_out: bfloat16 [8, 1024, 2048], P('dp', 'ctx'), may hold values from -6 to 6
Outputs:
- outputs: bfloat16 [8, 1024, 2048], P('dp', 'ctx')
- grad_inputs: float32 [8, 1024, 2048], P('dp', 'ctx')
- grad_norm_gain: float32 [2048], replicated
- grad_up_weight: float32 [2048, 8192], P('dp')
- grad_conv_weight: float32 [4, 4096], replicated
- grad_conv_bias: float32 [4096], replicated
- grad_qkv_weight: float32 [3, 4, 4, 4, 256], replicated
- grad_gate_weight: float32 [8, 12288], replicated
- grad_gate_bias: float32 [8], replicated
- grad_skip_weight: float32 [4096], replicated
- grad_outnorm_weight: float32 [4096], replicated
- grad_down_weight: float32 [4096, 2048], P('dp')
Inputs may be any that keep to these rules, and one draw needn't show every extreme that they name: `lengths`: each entry counts the real tokens of a sequence from its start; one sequence has exactly 1024, another exactly 512.
All inputs are finite; a program needn't handle non-finite values.
Results may differ from a plain program's by a relative error of at most 0.04.
Values may be sent and summed in bfloat16 or wider, within the bound.
No kernel may reach another device: no remote copies, remote signals or barrier semaphores. Data moves between devices by JAX's collectives and lax.ppermute only.
A program may use at most 448 MiB of HBM per device.

v0:
```python
from functools import partial
import jax
import jax.numpy as jnp
from jax import lax
from jax.sharding import PartitionSpec as P

highest = lax.Precision.HIGHEST
epsilon = 1e-05


def shifted(x, axis, by):
    length = lax.axis_size(axis)
    pairs = [(i, i + by) for i in range(length) if 0 <= i + by < length]
    return lax.ppermute(x, axis, pairs)


def low(value_in):
    rounded = lax.optimization_barrier(value_in.astype(jnp.bfloat16)).astype(jnp.float32)
    return value_in + lax.stop_gradient(rounded - value_in)


def layer_norm_low(rows_in, gain_row):
    centred = rows_in - jnp.mean(rows_in, axis=-1, keepdims=True)
    spread = jnp.mean(centred * centred, axis=-1, keepdims=True)
    return low(centred * lax.rsqrt(spread + epsilon) * gain_row)


def headwise(values_in, blocks_in):
    row_count, width_all = values_in.shape
    head_count, block_size, block_out, block_count = blocks_in.shape
    grouped = values_in.reshape(row_count, head_count, block_size, block_count)
    mixed_rows = jnp.einsum("thij,hioj->thoj", grouped, blocks_in, precision=highest)
    return mixed_rows.reshape(row_count, width_all)


def split_heads(rows_in, head_count):
    return rows_in.reshape(rows_in.shape[0], head_count, -1).transpose(1, 0, 2)


def mid_section(mixer_in, rim_rows, conv_taps, conv_shift, qkv_blocks, gate_matrix, gate_offset):
    row_count, width_all = mixer_in.shape
    kernel_size = conv_taps.shape[0]
    head_count = qkv_blocks.shape[1]
    padded_in = jnp.concatenate([rim_rows, mixer_in], axis=0)
    conv_pre = conv_shift[None, :] + conv_taps[0][None, :] * padded_in[0:row_count]
    for tap_index in range(1, kernel_size):
        conv_pre = (
            conv_pre + conv_taps[tap_index][None, :] * padded_in[tap_index : tap_index + row_count]
        )
    conv_out = jax.nn.silu(conv_pre)
    key_scale = (width_all // head_count) ** (-0.5)
    queries = low(headwise(conv_out, qkv_blocks[0]))
    key_rows = low(headwise(conv_out, qkv_blocks[1]) * key_scale)
    value_rows = low(headwise(mixer_in, qkv_blocks[2]))
    joined = jnp.concatenate([queries, key_rows, value_rows], axis=1)
    gate_pre = jnp.dot(joined, gate_matrix.T, precision=highest) + gate_offset[None, :]
    return (
        queries,
        key_rows,
        value_rows,
        gate_pre[:, :head_count],
        jax.nn.log_sigmoid(gate_pre[:, head_count:]),
        conv_out,
    )


def cell_scores(queries, key_rows, head_count):
    return jnp.einsum(
        "htk,hsk->hts",
        split_heads(queries, head_count),
        split_heads(key_rows, head_count),
        precision=highest,
    )


def cell_rest(scores, queries, value_rows, in_gate, log_forget, state_in):
    row_count, width_all = queries.shape
    head_count = state_in.shape[0]
    query_heads = split_heads(queries, head_count)
    value_heads = split_heads(value_rows, head_count)
    decay_sum = jnp.cumsum(log_forget, axis=0).T
    gate_row = in_gate.T
    causal = jnp.arange(row_count)[:, None] >= jnp.arange(row_count)[None, :]
    exponent = decay_sum[:, :, None] - decay_sum[:, None, :] + gate_row[:, None, :]
    weights = jnp.where(causal[None], jnp.exp(jnp.where(causal[None], exponent, 0.0)), 0.0)
    mix_weights = low(weights * scores)
    within = jnp.einsum("hts,hsd->htd", mix_weights, value_heads, precision=highest)
    carried = jnp.einsum("htk,hkd->htd", query_heads, low(state_in), precision=highest)
    numerator = within + jnp.exp(decay_sum)[:, :, None] * carried
    return numerator.transpose(1, 0, 2).reshape(row_count, width_all)


def summary(key_rows, value_rows, in_gate, log_forget):
    head_count = in_gate.shape[1]
    decay_sum = jnp.cumsum(log_forget, axis=0)
    span_decay = decay_sum[-1]
    weights = jnp.exp(span_decay[None, :] - decay_sum + in_gate)
    weighted = low(split_heads(key_rows, head_count) * weights.T[:, :, None])
    state_part = jnp.einsum(
        "htk,htd->hkd", weighted, split_heads(value_rows, head_count), precision=highest
    )
    return (state_part, span_decay)


def tail_section(numerator, conv_out, gate_in, outnorm_scale, skip_scale, head_count):
    row_count, width_all = numerator.shape
    grouped = numerator.reshape(row_count, head_count, -1)
    centred = grouped - jnp.mean(grouped, axis=-1, keepdims=True)
    spread = jnp.mean(centred * centred, axis=-1, keepdims=True)
    normed = (centred * lax.rsqrt(spread + epsilon)).reshape(row_count, width_all) * outnorm_scale
    return low((normed + skip_scale * conv_out) * jax.nn.silu(gate_in))


def on_device(
    inputs,
    lengths,
    norm_gain,
    up_weight,
    conv_weight,
    conv_bias,
    qkv_weight,
    gate_weight,
    gate_bias,
    skip_weight,
    outnorm_weight,
    down_weight,
    grad_out,
):
    span_len = inputs.shape[1]
    inner_width = conv_weight.shape[1]
    head_count = qkv_weight.shape[1]
    kernel_size = conv_weight.shape[0]
    ctx_count = lax.axis_size("ctx")
    ctx_index = lax.axis_index("ctx")
    positions = ctx_index * span_len + jnp.arange(span_len)
    live_rows = (positions < lengths[0]).astype(jnp.float32)[:, None]
    rows_in = inputs[0].astype(jnp.float32)
    norm_scale = norm_gain.astype(jnp.float32)
    conv_taps = conv_weight.astype(jnp.float32)
    conv_shift = conv_bias.astype(jnp.float32)
    qkv_blocks = qkv_weight.astype(jnp.float32)
    gate_matrix = gate_weight.astype(jnp.float32)
    gate_offset = gate_bias.astype(jnp.float32)
    skip_scale = skip_weight.astype(jnp.float32)
    outnorm_scale = outnorm_weight.astype(jnp.float32)
    contract_last = (((1,), (1,)), ((), ()))
    contract_first = (((0,), (0,)), ((), ()))
    normed, front_back = jax.vjp(layer_norm_low, rows_in, norm_scale)
    normed_low = normed.astype(jnp.bfloat16)
    columns = normed_low
    upward = jnp.dot(
        columns,
        lax.all_gather(up_weight, "dp", axis=0, tiled=True),
        preferred_element_type=jnp.float32,
    )
    mixer_low = upward[:, :inner_width].astype(jnp.bfloat16)
    mixer_in = mixer_low.astype(jnp.float32)
    gate_in = upward[:, inner_width:]
    rim_rows = shifted(mixer_low[span_len - kernel_size + 1 :], "ctx", 1).astype(jnp.float32)
    mid_result, mid_back = jax.vjp(
        mid_section, mixer_in, rim_rows, conv_taps, conv_shift, qkv_blocks, gate_matrix, gate_offset
    )
    queries, key_rows, value_rows, in_gate, log_forget, conv_out = mid_result
    summed, summary_back = jax.vjp(summary, key_rows, value_rows, in_gate, log_forget)
    state_part, span_decay = summed

    def relay(turn, carried):
        return shifted(jnp.exp(span_decay)[:, None, None] * carried + state_part, "ctx", 1)

    state_in = lax.fori_loop(0, ctx_count - 1, relay, jnp.zeros_like(state_part))
    scores, score_back = jax.vjp(partial(cell_scores, head_count=head_count), queries, key_rows)
    numerator, rest_back = jax.vjp(
        cell_rest, scores, queries, value_rows, in_gate, log_forget, state_in
    )
    hidden_state, tail_back = jax.vjp(
        partial(tail_section, head_count=head_count),
        numerator,
        conv_out,
        gate_in,
        outnorm_scale,
        skip_scale,
    )
    hidden_low = hidden_state.astype(jnp.bfloat16)
    columns = hidden_low
    branch = jnp.dot(
        columns,
        lax.all_gather(down_weight, "dp", axis=0, tiled=True),
        preferred_element_type=jnp.float32,
    )
    outputs = (live_rows * (rows_in + branch)).astype(jnp.bfloat16)[None]
    out_grad = grad_out[0].astype(jnp.float32) * live_rows
    branch_grad = out_grad.astype(jnp.bfloat16)
    hidden_grad = lax.dot_general(
        branch_grad,
        lax.all_gather(down_weight, "dp", axis=0, tiled=True),
        contract_last,
        preferred_element_type=jnp.float32,
    )
    numer_raw, conv_tail_grad, gate_in_grad, outnorm_grad, skip_grad = tail_back(hidden_grad)
    numer_low = numer_raw.astype(jnp.bfloat16)
    numer_grad = numer_low.astype(jnp.float32)
    scores_raw, query_part, value_grad, ingate_grad, forget_grad, state_grad = rest_back(numer_grad)
    query_extra, key_grad = score_back(scores_raw.astype(jnp.bfloat16).astype(jnp.float32))
    query_grad = query_part + query_extra

    def relay_back(turn, carried):
        return shifted(jnp.exp(span_decay)[:, None, None] * carried + state_grad, "ctx", -1)

    later_grad = lax.fori_loop(0, ctx_count - 1, relay_back, jnp.zeros_like(state_grad))
    decay_grad = jnp.exp(span_decay) * jnp.sum(later_grad * state_in, axis=(1, 2))
    later_rounded = later_grad.astype(jnp.bfloat16).astype(jnp.float32)
    key_extra, value_extra, ingate_extra, forget_extra = summary_back((later_rounded, decay_grad))
    mid_grads = mid_back(
        (
            query_grad,
            key_grad + key_extra,
            value_grad + value_extra,
            ingate_grad + ingate_extra,
            forget_grad + forget_extra,
            conv_tail_grad,
        )
    )
    (
        mixer_grad,
        rim_grad,
        conv_taps_grad,
        conv_shift_grad,
        qkv_grad,
        gate_matrix_grad,
        gate_offset_grad,
    ) = mid_grads
    rim_returned = shifted(rim_grad.astype(jnp.bfloat16), "ctx", -1).astype(rim_grad.dtype)
    mixer_grad = mixer_grad + jnp.pad(rim_returned, ((span_len - kernel_size + 1, 0), (0, 0)))
    upward_grad = jnp.concatenate([mixer_grad, gate_in_grad], axis=1).astype(jnp.bfloat16)
    normed_grad = lax.dot_general(
        upward_grad,
        lax.all_gather(up_weight, "dp", axis=0, tiled=True),
        contract_last,
        preferred_element_type=jnp.float32,
    )
    front_grad, norm_scale_grad = front_back(normed_grad)
    input_grad = (out_grad + front_grad)[None]
    columns = normed_low
    up_part = lax.psum_scatter(
        lax.dot_general(
            columns, upward_grad, contract_first, preferred_element_type=jnp.float32
        ).astype(jnp.bfloat16),
        "dp",
        scatter_dimension=0,
        tiled=True,
    )
    columns = hidden_low
    down_part = lax.psum_scatter(
        lax.dot_general(
            columns, branch_grad, contract_first, preferred_element_type=jnp.float32
        ).astype(jnp.bfloat16),
        "dp",
        scatter_dimension=0,
        tiled=True,
    )
    up_total, down_total = (
        lax.psum(up_part, "ctx").astype(jnp.float32),
        lax.psum(down_part, "ctx").astype(jnp.float32),
    )
    small_total = lax.psum(
        (
            norm_scale_grad,
            conv_taps_grad,
            conv_shift_grad,
            qkv_grad,
            gate_matrix_grad,
            gate_offset_grad,
            skip_grad,
            outnorm_grad,
        ),
        ("dp", "ctx"),
    )
    return (
        outputs,
        input_grad,
        small_total[0],
        up_total,
        small_total[1],
        small_total[2],
        small_total[3],
        small_total[4],
        small_total[5],
        small_total[6],
        small_total[7],
        down_total,
    )


def solution(mesh):
    return jax.shard_map(
        on_device,
        mesh=mesh,
        in_specs=(
            P("dp", "ctx", None),
            P("dp"),
            P(),
            P("dp", None),
            P(),
            P(),
            P(),
            P(),
            P(),
            P(),
            P(),
            P("dp", None),
            P("dp", "ctx", None),
        ),
        out_specs=(
            P("dp", "ctx", None),
            P("dp", "ctx", None),
            P(),
            P("dp", None),
            P(),
            P(),
            P(),
            P(),
            P(),
            P(),
            P(),
            P("dp", None),
        ),
        check_vma=False,
    )
```

profile of v0, /device:TPU:0, one launch (start us, length us, event | category | flops | bytes accessed | tf_op | source)
XLA Modules:
  0.0 3726.6 jit_solution(15394948117392416776)
XLA Ops:
  16.5 157.0 %all-gather.3.cloned.1.call-done = bf16[2048,8192]{1,0:T(8,128)(2,1)} async-done(((bf16[256,8192]{1,0:T(8,128)(2,1)}), bf16[2048,8192]{1,0:T(8,128)(2,1)}) %all-gather.3.cloned.1.call-update) | async-done | bytes 33554448 | tf_op jit(solution)/shard_map/all_gather | solution.py:153
  173.5 19.8 fusion.142
  214.1 51.2 %all-gather.5.cloned.1.call-done = bf16[4096,2048]{1,0:T(8,128)(2,1)} async-done(((bf16[512,2048]{1,0:T(8,128)(2,1)}), bf16[4096,2048]{1,0:T(8,128)(2,1)}) %all-gather.5.cloned.1.call-update) | async-done | bytes 16777232 | tf_op jit(solution)/shard_map/all_gather | solution.py:187
  357.9 29.3 fusion.54
  395.1 1142.1 %while.24 = (s32[]{:T(128)}, f32[4,1024,1024]{2,1,0:T(8,128)}, f32[4,1,1]{0,2,1:T(1,128)S(1)}, f32[4,1024,1024]{2,1,0:T(8,128)}, s32[]{:T(128)}) while((s32[]{:T(128)}, f32[4,1024,1024]{2,1,0:T(8,128)}, f32[4,1,1]{0,2,1:T(1,128)S(1)}, f32[4,1024,1024]{2,1,0:T(8,128)}, s32[]{:T(128)}) %tuple.133), condition=%wide.region_5.6_spmd, body=%wide.region_4.5_spmd.sunk | while | flops 8388610 | bytes 117440624 | solution.py:170
  421.7 354.4 %collective-permute-done = f32[4,1024,1024]{2,1,0:T(8,128)} collective-permute-done((f32[4,1024,1024]{2,1,0:T(8,128)}, f32[4,1024,1024]{2,1,0:T(8,128)}, u32[]{:S(2)}, u32[]{:S(2)}) %collective-permute-start) | collective-permute-done | bytes 16777248 | tf_op jit(solution)/shard_map/while/body/eval_jaxpr/ppermute | solution.py:14
  803.6 353.6 %collective-permute-done = f32[4,1024,1024]{2,1,0:T(8,128)} collective-permute-done((f32[4,1024,1024]{2,1,0:T(8,128)}, f32[4,1024,1024]{2,1,0:T(8,128)}, u32[]{:S(2)}, u32[]{:S(2)}) %collective-permute-start) | collective-permute-done | bytes 16777248 | tf_op jit(solution)/shard_map/while/body/eval_jaxpr/ppermute | solution.py:14
  1184.6 352.6 %collective-permute-done = f32[4,1024,1024]{2,1,0:T(8,128)} collective-permute-done((f32[4,1024,1024]{2,1,0:T(8,128)}, f32[4,1024,1024]{2,1,0:T(8,128)}, u32[]{:S(2)}, u32[]{:S(2)}) %collective-permute-start) | collective-permute-done | bytes 16777248 | tf_op jit(solution)/shard_map/while/body/eval_jaxpr/ppermute | solution.py:14
  1547.3 22.0 fusion.1
  1591.8 21.5 fusion
  1613.3 18.2 fusion.4
  1639.4 1136.2 %while.25 = (s32[]{:T(128)}, f32[4,1024,1024]{2,1,0:T(8,128)}, f32[4,1,1]{0,2,1:T(1,128)S(1)}, f32[4,1024,1024]{2,1,0:T(8,128)}, s32[]{:T(128)}) while((s32[]{:T(128)}, f32[4,1024,1024]{2,1,0:T(8,128)}, f32[4,1,1]{0,2,1:T(1,128)S(1)}, f32[4,1024,1024]{2,1,0:T(8,128)}, s32[]{:T(128)}) %tuple.134), condition=%wide.region_11.12_spmd, body=%wide.region_10.11_spmd.sunk | while | flops 8388610 | bytes 117440624 | solution.py:209
  1658.0 361.4 %collective-permute-done.1 = f32[4,1024,1024]{2,1,0:T(8,128)} collective-permute-done((f32[4,1024,1024]{2,1,0:T(8,128)}, f32[4,1024,1024]{2,1,0:T(8,128)}, u32[]{:S(2)}, u32[]{:S(2)}) %collective-permute-start.1) | collective-permute-done | bytes 16777248 | tf_op jit(solution)/shard_map/while/body/eval_jaxpr/ppermute | solution.py:14
  2019.4 17.3 multiply_add_fusion.11
  2038.0 360.0 %collective-permute-done.1 = f32[4,1024,1024]{2,1,0:T(8,128)} collective-permute-done((f32[4,1024,1024]{2,1,0:T(8,128)}, f32[4,1024,1024]{2,1,0:T(8,128)}, u32[]{:S(2)}, u32[]{:S(2)}) %collective-permute-start.1) | collective-permute-done | bytes 16777248 | tf_op jit(solution)/shard_map/while/body/eval_jaxpr/ppermute | solution.py:14
  2398.0 17.3 multiply_add_fusion.11
  2416.6 359.1 %collective-permute-done.1 = f32[4,1024,1024]{2,1,0:T(8,128)} collective-permute-done((f32[4,1024,1024]{2,1,0:T(8,128)}, f32[4,1024,1024]{2,1,0:T(8,128)}, u32[]{:S(2)}, u32[]{:S(2)}) %collective-permute-start.1) | collective-permute-done | bytes 16777248 | tf_op jit(solution)/shard_map/while/body/eval_jaxpr/ppermute | solution.py:14
  2802.9 18.8 fusion.36
  2958.3 20.6 multiply_reduce_fusion.1
  3052.4 17.5 convolution_convert_fusion
  3119.0 194.8 %reduce-scatter.3.cloned.1.call-done = bf16[256,8192]{1,0:T(8,128)(2,1)} async-done(((bf16[2048,8192]{1,0:T(8,128)(2,1)}), bf16[256,8192]{1,0:T(8,128)(2,1)}) %reduce-scatter.3.cloned.1.call-update) | async-done | bytes 4194320 | tf_op jit(solution)/shard_map/reduce_scatter | solution.py:244
  3342.9 41.4 %all-reduce.15 = (f32[2048]{0:T(1024)}, f32[4096]{0:T(1024)}, f32[8]{0:T(128)}, f32[4096]{0:T(1024)}, f32[4096]{0:T(1024)}) all-reduce(f32[2048]{0:T(1024)S(1)} %get-tuple-element.147, f32[4096]{0:T(1024)S(1)} %get-tuple-element.193, f32[8]{0:T(128)S(1)} %fusion.106, ...), channel_id=1, replica_groups=mesh['dp'=8,'ctx'=4] {'dp','ctx'}, use_global_device_ids=true, to_apply=%region_25.26 | all-reduce | flops 14344 | bytes 114752 | tf_op jit(solution)/shard_map/psum | solution.py:265
  3387.7 95.7 %all-reduce.21.cloned.1.call-done = (f32[4,4096]{1,0:T(4,128)}, f32[3,4,4,4,256]{2,3,4,1,0:T(4,128)}, f32[8,12288]{1,0:T(8,128)}) async-done(((f32[4,4096]{1,0:T(4,128)}, f32[3,4,4,4,256]{2,3,4,1,0:T(4,128)}, f32[8,12288]{1,0:T(8,128)}), (f32[4,4096]{1,0:T(4,128)}, f32[3,4,4,4,256]{2,3,4,1,0:T(4,128)}, f32[8,12288]{1,0:T(8,128)})) %all-reduce.21.cloned.1.call-update) | async-done | bytes 655376 | tf_op jit(solution)/shard_map/psum | solution.py:265
  3489.5 219.5 %all-reduce.23.cloned.1.call-done = (bf16[256,8192]{1,0:T(8,128)(2,1)}, bf16[512,2048]{1,0:T(8,128)(2,1)}) async-done(((bf16[256,8192]{1,0:T(8,128)(2,1)}, bf16[512,2048]{1,0:T(8,128)(2,1)}), (bf16[256,8192]{1,0:T(8,128)(2,1)}, bf16[512,2048]{1,0:T(8,128)(2,1)})) %all-reduce.23.cloned.1.call-update) | async-done | bytes 6291472 | tf_op jit(solution)/shard_map/psum | solution.py:262
  (359 shorter events, 607.7 us)
Async XLA Ops:
  7.2 321.9 %copy-start = (bf16[8,12288]{1,0:T(8,128)(2,1)S(1)}, bf16[8,12288]{1,0:T(8,128)(2,1)}, u32[]{:S(2)}) copy-start(bf16[8,12288]{1,0:T(8,128)(2,1)} %param.24) | copy-start | bytes 589828
  7.3 166.2 %all-gather.3.cloned.1.call-start = ((), (), s32[]{:S(2)}) async-start(), calls=%async_computation.2 | async-start | bytes 37748736 | tf_op jit(solution)/shard_map/all_gather | solution.py:153
  8.0 257.3 %all-gather.5.cloned.1.call-start = ((), (), s32[]{:S(2)}) async-start(), calls=%async_computation.3 | async-start | bytes 18874368 | tf_op jit(solution)/shard_map/all_gather | solution.py:187
  8.8 3110.2 %reduce-scatter.5.cloned.1.call-start = ((), (), s32[]{:S(2)}) async-start(), calls=%async_computation.5 | async-start | bytes 18874368 | tf_op jit(solution)/shard_map/reduce_scatter | solution.py:253
  10.0 255.3 %copy-start.71 = (f32[4096]{0:T(1024)}, f32[4096]{0:T(1024)S(1)}, u32[]{:S(2)}) copy-start(f32[4096]{0:T(1024)S(1)} %convert_element_type.162) | copy-start | bytes 49156
  14.3 195.9 %copy-start.36 = (bf16[1,4,4,4,256]{2,3,4,1,0:T(4,128)(2,1)}, bf16[1,4,4,4,256]{2,3,4,1,0:T(4,128)(2,1)S(1)}, u32[]{:S(2)}) copy-start(bf16[1,4,4,4,256]{2,3,4,1,0:T(4,128)(2,1)S(1)} %copy.127) | copy-start | bytes 98308
  16.4 265.1 %copy-start.61 = (f32[1,4096]{1,0:T(1,128)}, f32[1,4096]{1,0:T(1,128)S(1)}, u32[]{:S(2)}) copy-start(f32[1,4096]{1,0:T(1,128)S(1)} %get-tuple-element.212) | copy-start | bytes 49156
  16.4 265.1 %copy-start.63 = (f32[1,4096]{1,0:T(1,128)}, f32[1,4096]{1,0:T(1,128)S(1)}, u32[]{:S(2)}) copy-start(f32[1,4096]{1,0:T(1,128)S(1)} %get-tuple-element.213) | copy-start | bytes 49156
  16.4 265.1 %copy-start.65 = (f32[1,4096]{1,0:T(1,128)}, f32[1,4096]{1,0:T(1,128)S(1)}, u32[]{:S(2)}) copy-start(f32[1,4096]{1,0:T(1,128)S(1)} %get-tuple-element.214) | copy-start | bytes 49156
  16.5 265.1 %copy-start.67 = (f32[1,4096]{1,0:T(1,128)}, f32[1,4096]{1,0:T(1,128)S(1)}, u32[]{:S(2)}) copy-start(f32[1,4096]{1,0:T(1,128)S(1)} %get-tuple-element.215) | copy-start | bytes 49156
  194.8 86.7 %collective-permute-start.2 = (bf16[3,4096]{1,0:T(4,128)(2,1)}, bf16[3,4096]{1,0:T(4,128)(2,1)S(1)}, u32[]{:S(2)}, u32[]{:S(2)}) collective-permute-start(bf16[3,4096]{1,0:T(4,128)(2,1)} %slice.91), channel_id=1, source_target_pairs={{0,1},{1,2},{2,3},{4,5},{5,6},{6,7},{8,9},{9,10},{10,11},{12,13},{... | collective-permute-start | bytes 73736 | tf_op jit(solution)/shard_map/ppermute | solution.py:14
  354.7 1214.6 %copy-start.45 = (bf16[4,256,256]{2,1,0:T(8,128)(2,1)}, bf16[4,256,256]{2,1,0:T(8,128)(2,1)S(1)}, u32[]{:S(2)}) copy-start(bf16[4,256,256]{2,1,0:T(8,128)(2,1)S(1)} %get-tuple-element.229) | copy-start | bytes 1572868
  412.4 363.6 %collective-permute-start = (f32[4,1024,1024]{2,1,0:T(8,128)}, f32[4,1024,1024]{2,1,0:T(8,128)}, u32[]{:S(2)}, u32[]{:S(2)}) collective-permute-start(f32[4,1024,1024]{2,1,0:T(8,128)} %multiply_add_fusion.10), channel_id=1, source_target_pairs={{0,1},{1,2},{2,3},{4,5},{5,6},{6,7},{8,9},{9,10},{10,11},{12,13},{... | collective-permute-start | bytes 50331656 | tf_op jit(solution)/shard_map/while/body/eval_jaxpr/ppermute | solution.py:14
  793.3 363.8 %collective-permute-start = (f32[4,1024,1024]{2,1,0:T(8,128)}, f32[4,1024,1024]{2,1,0:T(8,128)}, u32[]{:S(2)}, u32[]{:S(2)}) collective-permute-start(f32[4,1024,1024]{2,1,0:T(8,128)} %multiply_add_fusion.10), channel_id=1, source_target_pairs={{0,1},{1,2},{2,3},{4,5},{5,6},{6,7},{8,9},{9,10},{10,11},{12,13},{... | collective-permute-start | bytes 50331656 | tf_op jit(solution)/shard_map/while/body/eval_jaxpr/ppermute | solution.py:14
  1174.4 362.8 %collective-permute-start = (f32[4,1024,1024]{2,1,0:T(8,128)}, f32[4,1024,1024]{2,1,0:T(8,128)}, u32[]{:S(2)}, u32[]{:S(2)}) collective-permute-start(f32[4,1024,1024]{2,1,0:T(8,128)} %multiply_add_fusion.10), channel_id=1, source_target_pairs={{0,1},{1,2},{2,3},{4,5},{5,6},{6,7},{8,9},{9,10},{10,11},{12,13},{... | collective-permute-start | bytes 50331656 | tf_op jit(solution)/shard_map/while/body/eval_jaxpr/ppermute | solution.py:14
  1656.7 362.7 %collective-permute-start.1 = (f32[4,1024,1024]{2,1,0:T(8,128)}, f32[4,1024,1024]{2,1,0:T(8,128)}, u32[]{:S(2)}, u32[]{:S(2)}) collective-permute-start(f32[4,1024,1024]{2,1,0:T(8,128)} %multiply_add_fusion.11), channel_id=1, source_target_pairs={{1,0},{2,1},{3,2},{5,4},{6,5},{7,6},{9,8},{10,9},{11,10},{13,12},{... | collective-permute-start | bytes 50331656 | tf_op jit(solution)/shard_map/while/body/eval_jaxpr/ppermute | solution.py:14
  2036.7 361.3 %collective-permute-start.1 = (f32[4,1024,1024]{2,1,0:T(8,128)}, f32[4,1024,1024]{2,1,0:T(8,128)}, u32[]{:S(2)}, u32[]{:S(2)}) collective-permute-start(f32[4,1024,1024]{2,1,0:T(8,128)} %multiply_add_fusion.11), channel_id=1, source_target_pairs={{1,0},{2,1},{3,2},{5,4},{6,5},{7,6},{9,8},{10,9},{11,10},{13,12},{... | collective-permute-start | bytes 50331656 | tf_op jit(solution)/shard_map/while/body/eval_jaxpr/ppermute | solution.py:14
  2415.3 360.4 %collective-permute-start.1 = (f32[4,1024,1024]{2,1,0:T(8,128)}, f32[4,1024,1024]{2,1,0:T(8,128)}, u32[]{:S(2)}, u32[]{:S(2)}) collective-permute-start(f32[4,1024,1024]{2,1,0:T(8,128)} %multiply_add_fusion.11), channel_id=1, source_target_pairs={{1,0},{2,1},{3,2},{5,4},{6,5},{7,6},{9,8},{10,9},{11,10},{13,12},{... | collective-permute-start | bytes 50331656 | tf_op jit(solution)/shard_map/while/body/eval_jaxpr/ppermute | solution.py:14
  2990.2 323.6 %reduce-scatter.3.cloned.1.call-start = ((), (), s32[]{:S(2)}) async-start(), calls=%async_computation.4 | async-start | bytes 37748736 | tf_op jit(solution)/shard_map/reduce_scatter | solution.py:244
  3023.8 22.4 collective-permute-start.3
  3069.9 413.6 %all-reduce.21.cloned.1.call-start = ((), (), s32[]{:S(2)}) async-start(), calls=%async_computation.6 | async-start | bytes 13500416 | tf_op jit(solution)/shard_map/psum | solution.py:265
  3118.7 195.2 %copy-start.35 = (bf16[256,4096]{1,0:T(8,128)(2,1)S(1)}, bf16[256,4096]{1,0:T(8,128)(2,1)}, u32[]{:S(2)}) copy-start(bf16[256,4096]{1,0:T(8,128)(2,1)} %copy-done.34) | copy-start | bytes 6291460
  3118.7 195.2 %copy-start.88 = (f32[256]{0:T(256)S(1)}, f32[256]{0:T(256)}, u32[]{:S(2)}) copy-start(f32[256]{0:T(256)} %compare_convert_fusion) | copy-start | bytes 3076
  3118.7 590.2 %all-reduce.23.cloned.1.call-start = ((), (), s32[]{:S(2)}) async-start(), calls=%async_computation.7 | async-start | bytes 12582912 | tf_op jit(solution)/shard_map/psum | solution.py:262
  (87 other events, 1463.6 us)
Sparse Core Ops, SparseCore 0:
  10.0 163.4 all-gather.2
  175.4 89.8 all-gather.4
  2990.3 114.7 reduce-scatter.4
  3108.5 205.2 reduce-scatter.2
  3321.5 161.8 all-reduce.20
  3485.8 223.0 all-reduce.22
where the time goes:
time: 3730 us
  waiting for transfers between devices  2860 us (77%)
  matrix products  346 us (9%)
  other arithmetic  244 us (7%)
  local copies, waits for them, and re-layouts  180 us (5%)
  blocking collectives  41.4 us (1%)
  starting transfers between devices  38.6 us (1%)
    ppermute x8, waiting for transfers between devices, shifted(): return lax.ppermute(x, axis, pairs)  2140 us
    psum x1, waiting for transfers between devices, on_device(): lax.psum(up_part, 'ctx').astype(jnp.float32)  219 us
    reduce_scatter x1, waiting for transfers between devices, on_device(): lax.psum_scatter(lax.dot_general(columns, upward_grad, contract_first, pr...  195 us
    all_gather x1, waiting for transfers between devices, on_device(): lax.all_gather(up_weight, 'dp', axis=0, tiled=True)  157 us
    psum x1, waiting for transfers between devices, on_device(): lax.psum((norm_scale_grad, conv_taps_grad, conv_shift_grad, qkv_grad, gat...  95.7 us
  transfers between devices with their start and end apart: 14, of which 11 were waited for; matrix products, arithmetic and copies ran while one was open for 6% of the time, Pallas kernels for 0%

commit v1 on v0

--- a/solution.py
+++ b/solution.py
@@ -262,19 +262,18 @@
         lax.psum(up_part, "ctx").astype(jnp.float32),
         lax.psum(down_part, "ctx").astype(jnp.float32),
     )
-    small_total = lax.psum(
-        (
-            norm_scale_grad,
-            conv_taps_grad,
-            conv_shift_grad,
-            qkv_grad,
-            gate_matrix_grad,
-            gate_offset_grad,
-            skip_grad,
-            outnorm_grad,
-        ),
-        ("dp", "ctx"),
-    )
+    small_total = (
+        norm_scale_grad,
+        conv_taps_grad,
+        conv_shift_grad,
+        qkv_grad,
+        gate_matrix_grad,
+        gate_offset_grad,
+        skip_grad,
+        outnorm_grad,
+    )
+    for mesh_axis in ("ctx", "dp"):
+        small_total = lax.psum(small_total, mesh_axis)
     return (
         outputs,
         input_grad,

time: 3730 us -> 3970 us (1.064)
  waiting for transfers between devices: 2860 us -> 3100 us
    reduce_scatter x1, waiting for transfers between devices: 0.02 us -> 118 us  [on_device(): lax.psum_scatter(lax.dot_general(columns, branch_grad, contract_first, pr...]
    psum x1 -> x2, waiting for transfers between devices: 95.7 us -> 201 us  [on_device(): small_total = lax.psum(small_total, mesh_axis)]
  transfers between devices with their start and end apart: 14 -> 15, of which waited for: 11 -> 13; matrix products, arithmetic and copies ran while one was open for 6% -> 4% of each run, Pallas kernels for 0% -> 0%
where the time goes in v1:
time: 3970 us; the launch traced here: 3960 us
  waiting for transfers between devices  3100 us (78%)
  matrix products  346 us (9%)
  other arithmetic  243 us (6%)
  local copies, waits for them, and re-layouts  178 us (4%)
  blocking collectives  43.7 us (1%)
    ppermute x8, waiting for transfers between devices, shifted(): return lax.ppermute(x, axis, pairs)  2140 us
    psum x1, waiting for transfers between devices, on_device(): lax.psum(up_part, 'ctx').astype(jnp.float32)  220 us
    reduce_scatter x1, waiting for transfers between devices, on_device(): lax.psum_scatter(lax.dot_general(columns, upward_grad, contract_first, pr...  209 us
    psum x2, waiting for transfers between devices, on_device(): small_total = lax.psum(small_total, mesh_axis)  201 us
    all_gather x1, waiting for transfers between devices, on_device(): lax.all_gather(up_weight, 'dp', axis=0, tiled=True)  157 us
    reduce_scatter x1, waiting for transfers between devices, on_device(): lax.psum_scatter(lax.dot_general(columns, branch_grad, contract_first, pr...  118 us
  transfers between devices with their start and end apart: 15, of which 13 were waited for; matrix products, arithmetic and copies ran while one was open for 4% of the time, Pallas kernels for 0%

profile of v1, /device:TPU:0, one launch (start us, length us, event | category | flops | bytes accessed | tf_op | source)
XLA Modules:
  0.0 3963.8 jit_solution(7765565035830504097)
XLA Ops:
  16.4 157.1 %all-gather.3.cloned.1.call-done = bf16[2048,8192]{1,0:T(8,128)(2,1)} async-done(((bf16[256,8192]{1,0:T(8,128)(2,1)}), bf16[2048,8192]{1,0:T(8,128)(2,1)}) %all-gather.3.cloned.1.call-update) | async-done | bytes 33554448 | tf_op jit(solution)/shard_map/all_gather | solution.py:153
  173.5 19.8 fusion.142
  214.1 51.2 %all-gather.5.cloned.1.call-done = bf16[4096,2048]{1,0:T(8,128)(2,1)} async-done(((bf16[512,2048]{1,0:T(8,128)(2,1)}), bf16[4096,2048]{1,0:T(8,128)(2,1)}) %all-gather.5.cloned.1.call-update) | async-done | bytes 16777232 | tf_op jit(solution)/shard_map/all_gather | solution.py:187
  357.6 29.2 fusion.54
  394.8 1142.1 %while.24 = (s32[]{:T(128)}, f32[4,1024,1024]{2,1,0:T(8,128)}, f32[4,1,1]{0,2,1:T(1,128)S(1)}, f32[4,1024,1024]{2,1,0:T(8,128)}, s32[]{:T(128)}) while((s32[]{:T(128)}, f32[4,1024,1024]{2,1,0:T(8,128)}, f32[4,1,1]{0,2,1:T(1,128)S(1)}, f32[4,1024,1024]{2,1,0:T(8,128)}, s32[]{:T(128)}) %tuple.136), condition=%wide.region_5.6_spmd, body=%wide.region_4.5_spmd.sunk | while | flops 8388610 | bytes 117440624 | solution.py:170
  421.3 354.4 %collective-permute-done = f32[4,1024,1024]{2,1,0:T(8,128)} collective-permute-done((f32[4,1024,1024]{2,1,0:T(8,128)}, f32[4,1024,1024]{2,1,0:T(8,128)}, u32[]{:S(2)}, u32[]{:S(2)}) %collective-permute-start) | collective-permute-done | bytes 16777248 | tf_op jit(solution)/shard_map/while/body/eval_jaxpr/ppermute | solution.py:14
  803.2 353.6 %collective-permute-done = f32[4,1024,1024]{2,1,0:T(8,128)} collective-permute-done((f32[4,1024,1024]{2,1,0:T(8,128)}, f32[4,1024,1024]{2,1,0:T(8,128)}, u32[]{:S(2)}, u32[]{:S(2)}) %collective-permute-start) | collective-permute-done | bytes 16777248 | tf_op jit(solution)/shard_map/while/body/eval_jaxpr/ppermute | solution.py:14
  1184.3 352.7 %collective-permute-done = f32[4,1024,1024]{2,1,0:T(8,128)} collective-permute-done((f32[4,1024,1024]{2,1,0:T(8,128)}, f32[4,1024,1024]{2,1,0:T(8,128)}, u32[]{:S(2)}, u32[]{:S(2)}) %collective-permute-start) | collective-permute-done | bytes 16777248 | tf_op jit(solution)/shard_map/while/body/eval_jaxpr/ppermute | solution.py:14
  1547.0 21.8 fusion.1
  1591.5 21.5 fusion
  1613.0 18.2 fusion.4
  1639.1 1136.3 %while.25 = (s32[]{:T(128)}, f32[4,1024,1024]{2,1,0:T(8,128)}, f32[4,1,1]{0,2,1:T(1,128)S(1)}, f32[4,1024,1024]{2,1,0:T(8,128)}, s32[]{:T(128)}) while((s32[]{:T(128)}, f32[4,1024,1024]{2,1,0:T(8,128)}, f32[4,1,1]{0,2,1:T(1,128)S(1)}, f32[4,1024,1024]{2,1,0:T(8,128)}, s32[]{:T(128)}) %tuple.137), condition=%wide.region_11.12_spmd, body=%wide.region_10.11_spmd.sunk | while | flops 8388610 | bytes 117440624 | solution.py:209
  1657.7 361.4 %collective-permute-done.1 = f32[4,1024,1024]{2,1,0:T(8,128)} collective-permute-done((f32[4,1024,1024]{2,1,0:T(8,128)}, f32[4,1024,1024]{2,1,0:T(8,128)}, u32[]{:S(2)}, u32[]{:S(2)}) %collective-permute-start.1) | collective-permute-done | bytes 16777248 | tf_op jit(solution)/shard_map/while/body/eval_jaxpr/ppermute | solution.py:14
  2037.7 360.0 %collective-permute-done.1 = f32[4,1024,1024]{2,1,0:T(8,128)} collective-permute-done((f32[4,1024,1024]{2,1,0:T(8,128)}, f32[4,1024,1024]{2,1,0:T(8,128)}, u32[]{:S(2)}, u32[]{:S(2)}) %collective-permute-start.1) | collective-permute-done | bytes 16777248 | tf_op jit(solution)/shard_map/while/body/eval_jaxpr/ppermute | solution.py:14
  2416.3 359.1 %collective-permute-done.1 = f32[4,1024,1024]{2,1,0:T(8,128)} collective-permute-done((f32[4,1024,1024]{2,1,0:T(8,128)}, f32[4,1024,1024]{2,1,0:T(8,128)}, u32[]{:S(2)}, u32[]{:S(2)}) %collective-permute-start.1) | collective-permute-done | bytes 16777248 | tf_op jit(solution)/shard_map/while/body/eval_jaxpr/ppermute | solution.py:14
  2802.4 18.7 fusion.36
  2995.3 20.3 multiply_reduce_fusion.1
  3115.3 163.1 %all-reduce.26.cloned.1.call-done = (f32[4,4096]{1,0:T(4,128)}, f32[3,4,4,4,256]{2,3,4,1,0:T(4,128)}, f32[8,12288]{1,0:T(8,128)}) async-done(((f32[4,4096]{1,0:T(4,128)}, f32[3,4,4,4,256]{2,3,4,1,0:T(4,128)}, f32[8,12288]{1,0:T(8,128)}), (f32[4,4096]{1,0:T(4,128)}, f32[3,4,4,4,256]{2,3,4,1,0:T(4,128)}, f32[8,12288]{1,0:T(8,128)})) %all-reduce.26.cloned.1.call-update) | async-done | bytes 655376 | tf_op jit(solution)/shard_map/psum | solution.py:276
  3278.6 118.4 %reduce-scatter.5.cloned.1.call-done = bf16[512,2048]{1,0:T(8,128)(2,1)} async-done(((bf16[4096,2048]{1,0:T(8,128)(2,1)}), bf16[512,2048]{1,0:T(8,128)(2,1)}) %reduce-scatter.5.cloned.1.call-update) | async-done | bytes 2097168 | tf_op jit(solution)/shard_map/reduce_scatter | solution.py:253
  3397.0 209.1 %reduce-scatter.3.cloned.1.call-done = bf16[256,8192]{1,0:T(8,128)(2,1)} async-done(((bf16[2048,8192]{1,0:T(8,128)(2,1)}), bf16[256,8192]{1,0:T(8,128)(2,1)}) %reduce-scatter.3.cloned.1.call-update) | async-done | bytes 4194320 | tf_op jit(solution)/shard_map/reduce_scatter | solution.py:244
  3635.0 19.7 all-reduce.17
  3654.7 24.0 all-reduce.15
  3682.1 38.0 all-reduce.24.cloned.1.call-done
  3726.2 219.7 %all-reduce.28.cloned.1.call-done = (bf16[256,8192]{1,0:T(8,128)(2,1)}, bf16[512,2048]{1,0:T(8,128)(2,1)}) async-done(((bf16[256,8192]{1,0:T(8,128)(2,1)}, bf16[512,2048]{1,0:T(8,128)(2,1)}), (bf16[256,8192]{1,0:T(8,128)(2,1)}, bf16[512,2048]{1,0:T(8,128)(2,1)})) %all-reduce.28.cloned.1.call-update) | async-done | bytes 6291472 | tf_op jit(solution)/shard_map/psum | solution.py:262
  (355 shorter events, 656.8 us)
Async XLA Ops:
  7.2 321.8 %copy-start = (bf16[8,12288]{1,0:T(8,128)(2,1)S(1)}, bf16[8,12288]{1,0:T(8,128)(2,1)}, u32[]{:S(2)}) copy-start(bf16[8,12288]{1,0:T(8,128)(2,1)} %param.24) | copy-start | bytes 589828
  7.3 166.2 %all-gather.3.cloned.1.call-start = ((), (), s32[]{:S(2)}) async-start(), calls=%async_computation.2 | async-start | bytes 37748736 | tf_op jit(solution)/shard_map/all_gather | solution.py:153
  8.0 257.3 %all-gather.5.cloned.1.call-start = ((), (), s32[]{:S(2)}) async-start(), calls=%async_computation.3 | async-start | bytes 18874368 | tf_op jit(solution)/shard_map/all_gather | solution.py:187
  8.8 3269.5 %all-reduce.26.cloned.1.call-start = ((), (), s32[]{:S(2)}) async-start(), calls=%async_computation.7 | async-start | bytes 13500416 | tf_op jit(solution)/shard_map/psum | solution.py:276
  10.0 255.3 %copy-start.73 = (f32[4096]{0:T(1024)}, f32[4096]{0:T(1024)S(1)}, u32[]{:S(2)}) copy-start(f32[4096]{0:T(1024)S(1)} %convert_element_type.162) | copy-start | bytes 49156
  14.3 195.7 %copy-start.35 = (bf16[1,4,4,4,256]{2,3,4,1,0:T(4,128)(2,1)}, bf16[1,4,4,4,256]{2,3,4,1,0:T(4,128)(2,1)S(1)}, u32[]{:S(2)}) copy-start(bf16[1,4,4,4,256]{2,3,4,1,0:T(4,128)(2,1)S(1)} %copy.127) | copy-start | bytes 98308
  16.4 265.2 %copy-start.63 = (f32[1,4096]{1,0:T(1,128)}, f32[1,4096]{1,0:T(1,128)S(1)}, u32[]{:S(2)}) copy-start(f32[1,4096]{1,0:T(1,128)S(1)} %get-tuple-element.220) | copy-start | bytes 49156
  16.4 265.2 %copy-start.65 = (f32[1,4096]{1,0:T(1,128)}, f32[1,4096]{1,0:T(1,128)S(1)}, u32[]{:S(2)}) copy-start(f32[1,4096]{1,0:T(1,128)S(1)} %get-tuple-element.221) | copy-start | bytes 49156
  16.4 265.2 %copy-start.67 = (f32[1,4096]{1,0:T(1,128)}, f32[1,4096]{1,0:T(1,128)S(1)}, u32[]{:S(2)}) copy-start(f32[1,4096]{1,0:T(1,128)S(1)} %get-tuple-element.222) | copy-start | bytes 49156
  16.4 265.2 %copy-start.69 = (f32[1,4096]{1,0:T(1,128)}, f32[1,4096]{1,0:T(1,128)S(1)}, u32[]{:S(2)}) copy-start(f32[1,4096]{1,0:T(1,128)S(1)} %get-tuple-element.223) | copy-start | bytes 49156
  194.8 86.7 %collective-permute-start.2 = (bf16[3,4096]{1,0:T(4,128)(2,1)}, bf16[3,4096]{1,0:T(4,128)(2,1)S(1)}, u32[]{:S(2)}, u32[]{:S(2)}) collective-permute-start(bf16[3,4096]{1,0:T(4,128)(2,1)} %slice.91), channel_id=1, source_target_pairs={{0,1},{1,2},{2,3},{4,5},{5,6},{6,7},{8,9},{9,10},{10,11},{12,13},{... | collective-permute-start | bytes 73736 | tf_op jit(solution)/shard_map/ppermute | solution.py:14
  354.5 1214.3 %copy-start.46 = (bf16[4,256,256]{2,1,0:T(8,128)(2,1)}, bf16[4,256,256]{2,1,0:T(8,128)(2,1)S(1)}, u32[]{:S(2)}) copy-start(bf16[4,256,256]{2,1,0:T(8,128)(2,1)S(1)} %get-tuple-element.237) | copy-start | bytes 1572868
  412.1 363.6 %collective-permute-start = (f32[4,1024,1024]{2,1,0:T(8,128)}, f32[4,1024,1024]{2,1,0:T(8,128)}, u32[]{:S(2)}, u32[]{:S(2)}) collective-permute-start(f32[4,1024,1024]{2,1,0:T(8,128)} %multiply_add_fusion.10), channel_id=1, source_target_pairs={{0,1},{1,2},{2,3},{4,5},{5,6},{6,7},{8,9},{9,10},{10,11},{12,13},{... | collective-permute-start | bytes 50331656 | tf_op jit(solution)/shard_map/while/body/eval_jaxpr/ppermute | solution.py:14
  793.0 363.8 %collective-permute-start = (f32[4,1024,1024]{2,1,0:T(8,128)}, f32[4,1024,1024]{2,1,0:T(8,128)}, u32[]{:S(2)}, u32[]{:S(2)}) collective-permute-start(f32[4,1024,1024]{2,1,0:T(8,128)} %multiply_add_fusion.10), channel_id=1, source_target_pairs={{0,1},{1,2},{2,3},{4,5},{5,6},{6,7},{8,9},{9,10},{10,11},{12,13},{... | collective-permute-start | bytes 50331656 | tf_op jit(solution)/shard_map/while/body/eval_jaxpr/ppermute | solution.py:14
  1174.1 362.9 %collective-permute-start = (f32[4,1024,1024]{2,1,0:T(8,128)}, f32[4,1024,1024]{2,1,0:T(8,128)}, u32[]{:S(2)}, u32[]{:S(2)}) collective-permute-start(f32[4,1024,1024]{2,1,0:T(8,128)} %multiply_add_fusion.10), channel_id=1, source_target_pairs={{0,1},{1,2},{2,3},{4,5},{5,6},{6,7},{8,9},{9,10},{10,11},{12,13},{... | collective-permute-start | bytes 50331656 | tf_op jit(solution)/shard_map/while/body/eval_jaxpr/ppermute | solution.py:14
  1656.4 362.7 %collective-permute-start.1 = (f32[4,1024,1024]{2,1,0:T(8,128)}, f32[4,1024,1024]{2,1,0:T(8,128)}, u32[]{:S(2)}, u32[]{:S(2)}) collective-permute-start(f32[4,1024,1024]{2,1,0:T(8,128)} %multiply_add_fusion.11), channel_id=1, source_target_pairs={{1,0},{2,1},{3,2},{5,4},{6,5},{7,6},{9,8},{10,9},{11,10},{13,12},{... | collective-permute-start | bytes 50331656 | tf_op jit(solution)/shard_map/while/body/eval_jaxpr/ppermute | solution.py:14
  2036.4 361.3 %collective-permute-start.1 = (f32[4,1024,1024]{2,1,0:T(8,128)}, f32[4,1024,1024]{2,1,0:T(8,128)}, u32[]{:S(2)}, u32[]{:S(2)}) collective-permute-start(f32[4,1024,1024]{2,1,0:T(8,128)} %multiply_add_fusion.11), channel_id=1, source_target_pairs={{1,0},{2,1},{3,2},{5,4},{6,5},{7,6},{9,8},{10,9},{11,10},{13,12},{... | collective-permute-start | bytes 50331656 | tf_op jit(solution)/shard_map/while/body/eval_jaxpr/ppermute | solution.py:14
  2415.0 360.4 %collective-permute-start.1 = (f32[4,1024,1024]{2,1,0:T(8,128)}, f32[4,1024,1024]{2,1,0:T(8,128)}, u32[]{:S(2)}, u32[]{:S(2)}) collective-permute-start(f32[4,1024,1024]{2,1,0:T(8,128)} %multiply_add_fusion.11), channel_id=1, source_target_pairs={{1,0},{2,1},{3,2},{5,4},{6,5},{7,6},{9,8},{10,9},{11,10},{13,12},{... | collective-permute-start | bytes 50331656 | tf_op jit(solution)/shard_map/while/body/eval_jaxpr/ppermute | solution.py:14
  3040.4 356.6 %reduce-scatter.5.cloned.1.call-start = ((), (), s32[]{:S(2)}) async-start(), calls=%async_computation.5 | async-start | bytes 18874368 | tf_op jit(solution)/shard_map/reduce_scatter | solution.py:253
  3052.1 554.1 %reduce-scatter.3.cloned.1.call-start = ((), (), s32[]{:S(2)}) async-start(), calls=%async_computation.4 | async-start | bytes 37748736 | tf_op jit(solution)/shard_map/reduce_scatter | solution.py:244
  3069.8 22.2 collective-permute-start.3
  3115.2 604.9 %all-reduce.24.cloned.1.call-start = ((), (), s32[]{:S(2)}) async-start(), calls=%async_computation.6 | async-start | bytes 13500416 | tf_op jit(solution)/shard_map/psum | solution.py:276
  3278.3 328.0 %copy-start.34 = (bf16[256,4096]{1,0:T(8,128)(2,1)S(1)}, bf16[256,4096]{1,0:T(8,128)(2,1)}, u32[]{:S(2)}) copy-start(bf16[256,4096]{1,0:T(8,128)(2,1)} %get-tuple-element.207) | copy-start | bytes 6291460
  3278.3 667.5 %all-reduce.28.cloned.1.call-start = ((), (), s32[]{:S(2)}) async-start(), calls=%async_computation.8 | async-start | bytes 12582912 | tf_op jit(solution)/shard_map/psum | solution.py:262
  (84 other events, 1399.5 us)
Sparse Core Ops, SparseCore 0:
  10.0 163.4 all-gather.2
  175.4 89.8 all-gather.4
  3040.5 237.7 all-reduce.25
  3282.1 114.8 reduce-scatter.4
  3400.8 205.2 reduce-scatter.2
  3609.6 110.4 all-reduce.23
  3722.5 223.2 all-reduce.27
